TPU v7x, 32 devices: a whole 2x2x4 slice. The times are simulated.
32 devices in a mesh: groups: 2 (over y), dp: 16 (over z, x, core).
Axes of the slice: x: 2, y: 2, z: 4, core: 2. Of those that a mesh axis runs over, the one named last changes fastest.
Arguments:
- queries: bfloat16 [96, 128, 2560], P(('groups', 'dp')), parts along dimension 0, may hold values from -50 to 50
- keys: bfloat16 [96, 128, 2560], P(('groups', 'dp')), parts along dimension 0, may hold values from -4 to 4
- values: bfloat16 [96, 128, 2560], P(('groups', 'dp')), parts along dimension 0, may hold values from -6 to 6
- counts: int32 [32], P(('groups', 'dp')), parts along dimension 0, may hold values from 1 to 3, as said below
- neighbours: int32 [96, 3], P(('groups', 'dp')), parts along dimension 0, may hold values from 0 to 5, as said below
- gate_table: float32 [50, 2560], replicated, may hold values from 1 to 8
- step: int32 [1], replicated, may hold values from 0 to 49
- out_weight: bfloat16 [2560, 5120], P(None, 'dp'), may hold values from -0.125 to 0.125
Outputs:
- mixed: bfloat16 [96, 128, 5120], P(('groups', 'dp')), parts along dimension 0
There are 2 independent parts, one for each index of `groups`. A program takes and returns all parts, laid end to end along the dimension named above; an argument that names none is the same for every part. Nothing has to cross between parts.
Inputs may be any that keep to these rules, and one draw needn't show every extreme that they name: `counts`: the live slots of a device come first. Member m holds the devices (m*4 + 4//2 + r) modulo the number of devices, r = 0 to 3, its tile list running through them in that order. Some device holds 3 live tiles. `neighbours`: row t (a tile of device d) names 3 places of device d's extended list: places 0 to 0 are tiles s to s+1 - 1 of device d-1 (around the axis) with s = max(counts[d-1]-1, 0), place 1+j is the device's slot j, places 1 + 3 onward are the first tiles of device d+1 (around the axis), and 5 names no tile. In a live tile's row the first entry is the tile itself and the others name distinct live tiles of the same member or no tile; rows of slots past the device's count name no tile at all.
All inputs are finite; a program needn't handle non-finite values.
Results may differ from a plain program's by a relative error of at most 0.0052.
Values may be sent and summed in bfloat16 or wider, within the bound.
A program may use at most 192 MiB of HBM per device.

v0:
```python
import math

import jax
import jax.numpy as jnp
from jax import lax
from jax.sharding import PartitionSpec as P

HEADS = 20
HALO = 1


masked_score = -1e30


def shifted(shard, axis, by):
    devices = lax.axis_size(axis)
    return lax.ppermute(shard, axis, [(i, (i + by) % devices) for i in range(devices)])


def attend_tile(query_tile, key_rows, value_rows, key_valid, gate_row):
    query_rows, channels = query_tile.shape
    head_dim = channels // HEADS
    queries_h = query_tile.reshape(query_rows, HEADS, head_dim)
    keys_h = key_rows.reshape(-1, HEADS, head_dim)
    values_h = value_rows.reshape(-1, HEADS, head_dim)
    scores = jnp.einsum("qhd,khd->hqk", queries_h, keys_h, preferred_element_type=jnp.float32) * (
        1.0 / math.sqrt(head_dim)
    )
    scores = jnp.where(key_valid[None, None, :], scores, masked_score)
    row_max = jnp.max(scores, axis=-1, keepdims=True)
    raw_weights = jnp.exp(scores - row_max)
    denominator = jnp.sum(raw_weights, axis=-1)
    weights = raw_weights.astype(jnp.bfloat16)
    summed = jnp.einsum("hqk,khd->qhd", weights, values_h, preferred_element_type=jnp.float32)
    summed = summed / jnp.transpose(denominator)[:, :, None]
    return (summed.reshape(query_rows, channels) * gate_row[None, :]).astype(jnp.bfloat16)


def on_device(queries, keys, values, counts, neighbours, gate_table, step, out_weight):
    slot_count, tile_rows, channels = queries.shape
    sentinel = slot_count + 2 * HALO
    own_count = counts[0]
    tail_start = jnp.maximum(own_count - HALO, 0)
    tail_block = jnp.stack(
        [
            lax.dynamic_slice_in_dim(keys, tail_start, HALO, 0),
            lax.dynamic_slice_in_dim(values, tail_start, HALO, 0),
        ]
    )
    lead_block = jnp.stack([keys[:HALO], values[:HALO]])
    from_before = shifted(tail_block, "dp", 1)
    from_after = shifted(lead_block, "dp", -1)
    zero_tile = jnp.zeros((1, tile_rows, channels), jnp.bfloat16)
    ext_keys = jnp.concatenate([from_before[0], keys, from_after[0], zero_tile], axis=0)
    ext_values = jnp.concatenate([from_before[1], values, from_after[1], zero_tile], axis=0)
    gate_row = lax.dynamic_index_in_dim(gate_table, step[0], 0, keepdims=False)

    def own_tile(slot_id, result):
        tile_index = lax.dynamic_index_in_dim(neighbours, slot_id, 0, keepdims=False)
        picked_keys = jnp.take(ext_keys, tile_index, axis=0).reshape(-1, channels)
        picked_values = jnp.take(ext_values, tile_index, axis=0).reshape(-1, channels)
        key_valid = jnp.repeat(tile_index != sentinel, tile_rows)
        query_tile = lax.dynamic_index_in_dim(queries, slot_id, 0, keepdims=False)
        computed = attend_tile(query_tile, picked_keys, picked_values, key_valid, gate_row)
        return lax.dynamic_update_index_in_dim(result, computed, slot_id, 0)

    attended = lax.fori_loop(0, own_count, own_tile, jnp.zeros_like(queries))
    flat_rows = attended.reshape(slot_count * tile_rows, channels)
    projected = jnp.dot(
        flat_rows,
        lax.all_gather(out_weight, "dp", axis=1, tiled=True),
        preferred_element_type=jnp.float32,
    )
    return projected.astype(jnp.bfloat16).reshape(slot_count, tile_rows, -1)


def solution(mesh):
    placed = (
        P(("groups", "dp"), None, None),
        P(("groups", "dp"), None, None),
        P(("groups", "dp"), None, None),
        P(("groups", "dp")),
        P(("groups", "dp"), None),
        P(),
        P(),
        P(None, "dp"),
    )
    return jax.shard_map(
        on_device,
        mesh=mesh,
        in_specs=placed,
        out_specs=P(("groups", "dp"), None, None),
        check_vma=False,
    )
```

profile of v0, /device:TPU:5, one launch (start us, length us, event | category | flops | bytes accessed | tf_op | source)
XLA Modules:
  0.0 203.4 jit_solution(9878305853602540048)
XLA Ops:
  14.7 47.8 %collective-permute-done = bf16[2,1,128,2560]{3,2,1,0:T(8,128)(2,1)S(1)} collective-permute-done((bf16[2,1,128,2560]{3,2,1,0:T(8,128)(2,1)}, bf16[2,1,128,2560]{3,2,1,0:T(8,128)(2,1)S(1)}, u32[]{:S(2)}, u32[]{:S(2)}) %collective-permute-start) | collective-permute-done | bytes 1310752 | tf_op jit(solution)/shard_map/ppermute | solution.py:17
  62.6 10.6 %collective-permute-done.1 = bf16[2,1,128,2560]{3,2,1,0:T(8,128)(2,1)S(1)} collective-permute-done((bf16[2,1,128,2560]{3,2,1,0:T(8,128)(2,1)}, bf16[2,1,128,2560]{3,2,1,0:T(8,128)(2,1)S(1)}, u32[]{:S(2)}, u32[]{:S(2)}) %collective-permute-start.1) | collective-permute-done | bytes 1310752 | tf_op jit(solution)/shard_map/ppermute | solution.py:17
  73.3 3.8 %maximum_maximum_fusion.1 = (bf16[6,128,2560]{2,1,0:T(8,128)(2,1)}, bf16[6,128,2560]{2,1,0:T(8,128)(2,1)}) fusion(bf16[1,128,2560]{2,1,0:T(8,128)(2,1)S(1)} %get-tuple-element.87, bf16[3,128,2560]{2,1,0:T(8,128)(2,1)S(1)} %copy-done.5, bf16[1,128,2560]{2,1,0:T(8,128)(2,1)S(1)} %get-tuple-element.85, bf16[6]{0:T(256)(128)(2,1)S(1)} %pad.7.clone, ...), kind=kLoop, calls=%fused_computation.34 | loop fusion | flops 11796480 | bytes 14417932 | tf_op jit(solution)/shard_map/concatenate | solution.py:54
  78.6 100.8 %while.10 = (s32[]{:T(128)}, bf16[3,128,2560]{2,1,0:T(8,128)(2,1)}, s32[]{:T(128)}, s32[3,3]{1,0:T(4,128)}, bf16[6,128,2560]{2,1,0:T(8,128)(2,1)}, /*index=5*/bf...) while((s32[]{:T(128)}, bf16[3,128,2560]{2,1,0:T(8,128)(2,1)}, ...), condition=%wide.region_3.5_spmd, body=%wide.region_0.4_spmd.sunk | while | flops 517074976 | bytes 72156944 | solution.py:67
  79.9 3.0 %gather_fusion = bf16[3,128,2560]{2,1,0:T(8,128)(2,1)S(1)} fusion(bf16[6,128,2560]{2,1,0:T(8,128)(2,1)} %get-tuple-element.183, s32[1024]{0:T(1024)S(1)} %pad_clamp_fusion.2), kind=kCustom, calls=%fused_computation.clone.clone.1 | custom fusion | bytes 3932172 | tf_op jit(solution)/shard_map/while/body/jit(_take)/gather | solution.py:61
  82.9 4.1 %gather_fusion.1 = bf16[3,128,2560]{2,1,0:T(8,128)(2,1)} fusion(bf16[6,128,2560]{2,1,0:T(8,128)(2,1)} %get-tuple-element.185, s32[1024]{0:T(1024)S(1)} %pad_clamp_fusion.2), kind=kCustom, calls=%fused_computation.1.clone.clone.1 | custom fusion | bytes 3932172 | tf_op jit(solution)/shard_map/while/body/jit(_take)/gather | solution.py:60
  87.0 3.9 %broadcast_select_fusion.3 = (bf16[3,128,2560]{2,1,0:T(8,128)(2,1)}, bf16[3,128,2560]{2,1,0:T(8,128)(2,1)}) fusion(bf16[3,128,2560]{2,1,0:T(8,128)(2,1)S(1)} %gather_fusion, pred[3]{0:T(512)(128)(4,1)S(1)} %get-tuple-element.152, bf16[3,128,2560]{2,1,0:T(8,128)(2,1)} %gather_fusion.1), kind=kLoop, calls=%fused_computation.15.clone.1 | loop fusion | flops 1966080 | bytes 7864323 | tf_op jit(solution)/shard_map/while/body/jit(_take)/select_n | solution.py:61
  90.9 3.0 %reshape.99 = bf16[384,20,128]{2,1,0:T(8,128)(2,1)S(1)} reshape(bf16[3,128,2560]{2,1,0:T(8,128)(2,1)} %get-tuple-element.153) | data formatting | bytes 3932160 | tf_op jit(solution)/shard_map/while/body/reshape;while/body/reshape | solution.py:24
  98.2 2.4 %fusion.39 = (f32[20,128]{1,0:T(8,128)S(1)}, f32[20,128,384]{2,1,0:T(8,128)S(1)}) fusion(pred[384]{0:T(512)(128)(4,1)S(1)} %broadcast_bitcast_fusion.2, bf16[128,20,128]{0,2,1:T(8,128)(2,1)} %bitcast.59, bf16[384,20,128]{2,1,0:T(8,128)(2,1)S(1)} %reshape.99), kind=kOutput, calls=%fused_computation.4.clone.1 | convolution fusion | flops 254604800 | bytes 6564224 | tf_op jit(solution)/shard_map/while/body/qhd,khd->hqk/dot_general | solution.py:26
  103.6 2.6 %reshape.100 = bf16[384,20,128]{2,1,0:T(8,128)(2,1)} reshape(bf16[3,128,2560]{2,1,0:T(8,128)(2,1)S(1)} %copy-done.3) | data formatting | bytes 3932160 | tf_op jit(solution)/shard_map/while/body/reshape;while/body/reshape | solution.py:25
  106.2 4.5 %fusion.41 = f32[128,20,128]{0,2,1:T(8,128)S(1)} fusion(f32[20,128,384]{2,1,0:T(8,128)} %copy-done.2, f32[20,128]{1,0:T(8,128)S(1)} %get-tuple-element.155, pred[384]{0:T(512)(128)(4,1)S(1)} %broadcast_bitcast_fusion.2, bf16[384,20,128]{2,1,0:T(8,128)(2,1)} %reshape.100, f32[128,20]{0,1:T(8,128)S(1)} %bitcast.61), kind=kOutput, calls=%fused_computation.20.clone.1 | convolution fusion | flops 255918080 | bytes 7229824 | tf_op jit(solution)/shard_map/while/body/hqk,khd->qhd/dot_general | solution.py:34
  113.6 2.8 %gather_fusion = bf16[3,128,2560]{2,1,0:T(8,128)(2,1)S(1)} fusion(bf16[6,128,2560]{2,1,0:T(8,128)(2,1)} %get-tuple-element.183, s32[1024]{0:T(1024)S(1)} %pad_clamp_fusion.2), kind=kCustom, calls=%fused_computation.clone.clone.1 | custom fusion | bytes 3932172 | tf_op jit(solution)/shard_map/while/body/jit(_take)/gather | solution.py:61
  116.4 4.2 %gather_fusion.1 = bf16[3,128,2560]{2,1,0:T(8,128)(2,1)} fusion(bf16[6,128,2560]{2,1,0:T(8,128)(2,1)} %get-tuple-element.185, s32[1024]{0:T(1024)S(1)} %pad_clamp_fusion.2), kind=kCustom, calls=%fused_computation.1.clone.clone.1 | custom fusion | bytes 3932172 | tf_op jit(solution)/shard_map/while/body/jit(_take)/gather | solution.py:60
  120.6 3.9 %broadcast_select_fusion.3 = (bf16[3,128,2560]{2,1,0:T(8,128)(2,1)}, bf16[3,128,2560]{2,1,0:T(8,128)(2,1)}) fusion(bf16[3,128,2560]{2,1,0:T(8,128)(2,1)S(1)} %gather_fusion, pred[3]{0:T(512)(128)(4,1)S(1)} %get-tuple-element.152, bf16[3,128,2560]{2,1,0:T(8,128)(2,1)} %gather_fusion.1), kind=kLoop, calls=%fused_computation.15.clone.1 | loop fusion | flops 1966080 | bytes 7864323 | tf_op jit(solution)/shard_map/while/body/jit(_take)/select_n | solution.py:61
  124.5 3.1 %reshape.99 = bf16[384,20,128]{2,1,0:T(8,128)(2,1)S(1)} reshape(bf16[3,128,2560]{2,1,0:T(8,128)(2,1)} %get-tuple-element.153) | data formatting | bytes 3932160 | tf_op jit(solution)/shard_map/while/body/reshape;while/body/reshape | solution.py:24
  137.1 2.6 %reshape.100 = bf16[384,20,128]{2,1,0:T(8,128)(2,1)} reshape(bf16[3,128,2560]{2,1,0:T(8,128)(2,1)S(1)} %copy-done.3) | data formatting | bytes 3932160 | tf_op jit(solution)/shard_map/while/body/reshape;while/body/reshape | solution.py:25
  139.7 4.3 %fusion.41 = f32[128,20,128]{0,2,1:T(8,128)S(1)} fusion(f32[20,128,384]{2,1,0:T(8,128)} %copy-done.2, f32[20,128]{1,0:T(8,128)S(1)} %get-tuple-element.155, pred[384]{0:T(512)(128)(4,1)S(1)} %broadcast_bitcast_fusion.2, bf16[384,20,128]{2,1,0:T(8,128)(2,1)} %reshape.100, f32[128,20]{0,1:T(8,128)S(1)} %bitcast.61), kind=kOutput, calls=%fused_computation.20.clone.1 | convolution fusion | flops 255918080 | bytes 7229824 | tf_op jit(solution)/shard_map/while/body/hqk,khd->qhd/dot_general | solution.py:34
  146.9 2.9 %gather_fusion = bf16[3,128,2560]{2,1,0:T(8,128)(2,1)S(1)} fusion(bf16[6,128,2560]{2,1,0:T(8,128)(2,1)} %get-tuple-element.183, s32[1024]{0:T(1024)S(1)} %pad_clamp_fusion.2), kind=kCustom, calls=%fused_computation.clone.clone.1 | custom fusion | bytes 3932172 | tf_op jit(solution)/shard_map/while/body/jit(_take)/gather | solution.py:61
  149.8 4.2 %gather_fusion.1 = bf16[3,128,2560]{2,1,0:T(8,128)(2,1)} fusion(bf16[6,128,2560]{2,1,0:T(8,128)(2,1)} %get-tuple-element.185, s32[1024]{0:T(1024)S(1)} %pad_clamp_fusion.2), kind=kCustom, calls=%fused_computation.1.clone.clone.1 | custom fusion | bytes 3932172 | tf_op jit(solution)/shard_map/while/body/jit(_take)/gather | solution.py:60
  154.0 3.8 %broadcast_select_fusion.3 = (bf16[3,128,2560]{2,1,0:T(8,128)(2,1)}, bf16[3,128,2560]{2,1,0:T(8,128)(2,1)}) fusion(bf16[3,128,2560]{2,1,0:T(8,128)(2,1)S(1)} %gather_fusion, pred[3]{0:T(512)(128)(4,1)S(1)} %get-tuple-element.152, bf16[3,128,2560]{2,1,0:T(8,128)(2,1)} %gather_fusion.1), kind=kLoop, calls=%fused_computation.15.clone.1 | loop fusion | flops 1966080 | bytes 7864323 | tf_op jit(solution)/shard_map/while/body/jit(_take)/select_n | solution.py:61
  157.8 3.0 %reshape.99 = bf16[384,20,128]{2,1,0:T(8,128)(2,1)S(1)} reshape(bf16[3,128,2560]{2,1,0:T(8,128)(2,1)} %get-tuple-element.153) | data formatting | bytes 3932160 | tf_op jit(solution)/shard_map/while/body/reshape;while/body/reshape | solution.py:24
  170.3 2.6 %reshape.100 = bf16[384,20,128]{2,1,0:T(8,128)(2,1)} reshape(bf16[3,128,2560]{2,1,0:T(8,128)(2,1)S(1)} %copy-done.3) | data formatting | bytes 3932160 | tf_op jit(solution)/shard_map/while/body/reshape;while/body/reshape | solution.py:25
  172.9 4.3 %fusion.41 = f32[128,20,128]{0,2,1:T(8,128)S(1)} fusion(f32[20,128,384]{2,1,0:T(8,128)} %copy-done.2, f32[20,128]{1,0:T(8,128)S(1)} %get-tuple-element.155, pred[384]{0:T(512)(128)(4,1)S(1)} %broadcast_bitcast_fusion.2, bf16[384,20,128]{2,1,0:T(8,128)(2,1)} %reshape.100, f32[128,20]{0,1:T(8,128)S(1)} %bitcast.61), kind=kOutput, calls=%fused_computation.20.clone.1 | convolution fusion | flops 255918080 | bytes 7229824 | tf_op jit(solution)/shard_map/while/body/hqk,khd->qhd/dot_general | solution.py:34
  179.4 17.2 %convolution_convert_fusion = bf16[384,5120]{1,0:T(8,128)(2,1)} fusion(bf16[384,2560]{1,0:T(8,128)(2,1)} %bitcast.60, bf16[2560,5120]{0,1:T(8,128)(2,1)} %all-gather.2.cloned.1.call-done), kind=kOutput, calls=%fused_computation.32 | convolution fusion | flops 10068295680 | bytes 32112640 | tf_op jit(solution)/shard_map/dot_general | solution.py:69
  (62 shorter events, 41.3 us)
Async XLA Ops:
  6.5 8.1 %copy-start = (f32[50,2560]{1,0:T(8,128)S(1)}, f32[50,2560]{1,0:T(8,128)}, u32[]{:S(2)}) copy-start(f32[50,2560]{1,0:T(8,128)} %param.17) | copy-start | bytes 1536004
  6.5 172.9 %all-gather.2.cloned.1.call-start = ((), (), s32[]{:S(2)}) async-start(), calls=%async_computation | async-start | bytes 27852800 | tf_op jit(solution)/shard_map/all_gather | solution.py:71
  11.0 51.5 %collective-permute-start = (bf16[2,1,128,2560]{3,2,1,0:T(8,128)(2,1)}, bf16[2,1,128,2560]{3,2,1,0:T(8,128)(2,1)S(1)}, u32[]{:S(2)}, u32[]{:S(2)}) collective-permute-start(bf16[2,1,128,2560]{3,2,1,0:T(8,128)(2,1)} %pad_maximum_fusion), channel_id=1, source_target_pairs={{0,1},{1,2},{2,3},{3,4},{4,5},{5,6},{6,7},{7,8},{8,9},{9,10},{10,1... | collective-permute-start | bytes 3932168 | tf_op jit(solution)/shard_map/ppermute | solution.py:17
  13.9 59.3 %collective-permute-start.1 = (bf16[2,1,128,2560]{3,2,1,0:T(8,128)(2,1)}, bf16[2,1,128,2560]{3,2,1,0:T(8,128)(2,1)S(1)}, u32[]{:S(2)}, u32[]{:S(2)}) collective-permute-start(bf16[2,1,128,2560]{3,2,1,0:T(8,128)(2,1)} %pad_maximum_fusion.1), channel_id=1, source_target_pairs={{0,15},{1,0},{2,1},{3,2},{4,3},{5,4},{6,5},{7,6},{8,7},{9,8},{10,9... | collective-permute-start | bytes 3932168 | tf_op jit(solution)/shard_map/ppermute | solution.py:17
  62.5 10.8 %copy-start.5 = (bf16[3,128,2560]{2,1,0:T(8,128)(2,1)S(1)}, bf16[3,128,2560]{2,1,0:T(8,128)(2,1)}, u32[]{:S(2)}) copy-start(bf16[3,128,2560]{2,1,0:T(8,128)(2,1)} %param.13) | copy-start | bytes 5898244
  62.6 10.8 %copy-start.4 = (bf16[3,128,2560]{2,1,0:T(8,128)(2,1)S(1)}, bf16[3,128,2560]{2,1,0:T(8,128)(2,1)}, u32[]{:S(2)}) copy-start(bf16[3,128,2560]{2,1,0:T(8,128)(2,1)} %param.14) | copy-start | bytes 5898244
  100.6 2.0 copy-start.2
  100.6 3.0 %copy-start.3 = (bf16[3,128,2560]{2,1,0:T(8,128)(2,1)S(1)}, bf16[3,128,2560]{2,1,0:T(8,128)(2,1)}, u32[]{:S(2)}) copy-start(bf16[3,128,2560]{2,1,0:T(8,128)(2,1)} %get-tuple-element.156) | copy-start | bytes 5898244 | tf_op jit(solution)/shard_map/while
  134.1 2.0 copy-start.2
  134.1 3.0 %copy-start.3 = (bf16[3,128,2560]{2,1,0:T(8,128)(2,1)S(1)}, bf16[3,128,2560]{2,1,0:T(8,128)(2,1)}, u32[]{:S(2)}) copy-start(bf16[3,128,2560]{2,1,0:T(8,128)(2,1)} %get-tuple-element.156) | copy-start | bytes 5898244 | tf_op jit(solution)/shard_map/while
  167.3 2.0 copy-start.2
  167.3 3.0 %copy-start.3 = (bf16[3,128,2560]{2,1,0:T(8,128)(2,1)S(1)}, bf16[3,128,2560]{2,1,0:T(8,128)(2,1)}, u32[]{:S(2)}) copy-start(bf16[3,128,2560]{2,1,0:T(8,128)(2,1)} %get-tuple-element.156) | copy-start | bytes 5898244 | tf_op jit(solution)/shard_map/while
  179.4 17.2 %copy-start.1 = (f32[50,2560]{1,0:T(8,128)S(1)}, f32[50,2560]{1,0:T(8,128)}, u32[]{:S(2)}) copy-start(f32[50,2560]{1,0:T(8,128)} %param.17) | copy-start | bytes 1536004
Sparse Core Ops, SparseCore 0:
  8.9 161.0 all-gather.1
where the time goes:
time: 205 us; the launch traced here: 203 us
  local copies, waits for them, and re-layouts  62.3 us (30%)
  waiting for transfers between devices  59.2 us (29%)
  matrix products  37.2 us (18%)
  other arithmetic  25.4 us (12%)
  between operations  14.8 us (7%)
  loops' own time  2.84 us (1%)
    ppermute x2, waiting for transfers between devices, shifted(): lax.ppermute(shard, axis, [(i, (i + by) % devices) for i in range(devices)])  58.4 us
    dot_general x1, matrix products, on_device(): jnp.dot(flat_rows, lax.all_gather(out_weight, 'dp', axis=1, tiled=True),...  17.2 us
    dot_general x3, matrix products, attend_tile(): jnp.einsum('hqk,khd->qhd', weights, values_h, preferred_element_type=jnp....  13.1 us
    gather x3, local copies, waits for them, and re-layouts, own_tile(): picked_keys = jnp.take(ext_keys, tile_index, axis=0).reshape(-1, channels)  12.5 us
    dynamic_slice x6, local copies, waits for them, and re-layouts, own_tile(): query_tile = lax.dynamic_index_in_dim(queries, slot_id, 0, keepdims=False)  12.4 us
    select_n x3, other arithmetic, own_tile(): jnp.take(ext_values, tile_index, axis=0).reshape(-1, channels)  11.6 us
    reshape x3, local copies, waits for them, and re-layouts, attend_tile(): keys_h = key_rows.reshape(-1, HEADS, head_dim)  9.19 us
    gather x3, local copies, waits for them, and re-layouts, own_tile(): jnp.take(ext_values, tile_index, axis=0).reshape(-1, channels)  8.61 us
  transfers between devices with their start and end apart: 3, of which 2 were waited for; matrix products, arithmetic and copies ran while one was open for 51% of the time, Pallas kernels for 0%

commit v1 on v0

--- a/solution.py
+++ b/solution.py
@@ -1,8 +1,11 @@
+import functools
 import math
 
 import jax
 import jax.numpy as jnp
 from jax import lax
+from jax.experimental import pallas as pl
+from jax.experimental.pallas import tpu as pltpu
 from jax.sharding import PartitionSpec as P
 
 HEADS = 20
@@ -74,6 +77,339 @@
     return projected.astype(jnp.bfloat16).reshape(slot_count, tile_rows, -1)
 
 
+MESH = pl.DeviceIdType.MESH
+NT = (((1,), (1,)), ((), ()))
+UP, DOWN, ACROSS, OVER, PARTNER = range(5)
+
+
+def fused(
+    planes,
+    keys_hbm,
+    values_hbm,
+    queries_hbm,
+    tail_keys,
+    tail_values,
+    weight_hbm,
+    gates_ref,
+    bias_ref,
+    places_ref,
+    out_ref,
+    ext_keys,
+    ext_values,
+    held_queries,
+    attended,
+    gathered,
+    load_sem,
+    halo_send,
+    halo_recv,
+    send_sem,
+    class_recv,
+    pair_recv,
+):
+    slots, rows, channels = held_queries.shape
+    half = channels // 2
+    head_dim = channels // HEADS
+    devices = planes * 4
+    group = lax.axis_index("groups")
+    me = lax.axis_index("dp")
+    core = lax.rem(me, 2)
+    x = lax.rem(lax.div(me, 2), 2)
+    z = lax.div(me, 4)
+    after = lax.rem(me + 1, devices)
+    before = lax.rem(me + devices - 1, devices)
+    has_up = z < planes - 1
+    has_down = z > 0
+    targets = {
+        UP: {"dp": me + 4},
+        DOWN: {"dp": me - 4},
+        ACROSS: {"dp": me + 2 - 4 * x},
+        OVER: {"groups": 1 - group},
+        PARTNER: {"dp": me + 1 - 2 * core},
+    }
+
+    loads = [
+        pltpu.make_async_copy(weight_hbm.at[h], gathered.at[z * 2 + x, h, core], load_sem.at[h])
+        for h in range(2)
+    ]
+    loads += [
+        pltpu.make_async_copy(keys_hbm, ext_keys.at[pl.ds(HALO, slots)], load_sem.at[2]),
+        pltpu.make_async_copy(values_hbm, ext_values.at[pl.ds(HALO, slots)], load_sem.at[3]),
+        pltpu.make_async_copy(queries_hbm, held_queries, load_sem.at[4]),
+    ]
+    for load in loads:
+        load.start()
+
+    barrier = pltpu.get_barrier_semaphore()
+
+    def greet(device):
+        pl.semaphore_signal(barrier, inc=1, device_id=device, device_id_type=MESH)
+
+    greet({"dp": after})
+    greet({"dp": before})
+    greet(targets[ACROSS])
+    greet(targets[OVER])
+    greet(targets[PARTNER])
+    pl.when(has_up)(lambda: greet(targets[UP]))
+    pl.when(has_down)(lambda: greet(targets[DOWN]))
+    pl.semaphore_wait(barrier, 5 + has_up.astype(jnp.int32) + has_down.astype(jnp.int32))
+
+    def halo(i, src, dst, device):
+        return pltpu.make_async_remote_copy(
+            src_ref=src,
+            dst_ref=dst,
+            send_sem=halo_send.at[i],
+            recv_sem=halo_recv.at[i],
+            device_id={"dp": device},
+            device_id_type=MESH,
+        )
+
+    halos = [
+        halo(0, tail_keys, ext_keys.at[pl.ds(0, HALO)], after),
+        halo(1, keys_hbm.at[pl.ds(0, HALO)], ext_keys.at[pl.ds(HALO + slots, HALO)], before),
+        halo(2, tail_values, ext_values.at[pl.ds(0, HALO)], after),
+        halo(3, values_hbm.at[pl.ds(0, HALO)], ext_values.at[pl.ds(HALO + slots, HALO)], before),
+    ]
+    for copy in halos:
+        copy.start()
+
+    def hop(route, chip, h):
+        piece = gathered.at[chip, h, core]
+        recv = pair_recv if route == PARTNER else class_recv
+        return pltpu.make_async_remote_copy(
+            src_ref=piece,
+            dst_ref=piece,
+            send_sem=send_sem.at[route, chip, h],
+            recv_sem=recv.at[chip, h],
+            device_id=targets[route],
+            device_id_type=MESH,
+        )
+
+    def arrive(chip, h):
+        hop(ACROSS, chip, h).wait_recv()
+
+    def arrive_pair(chip, h):
+        piece = gathered.at[chip, h, 1 - core]
+        pltpu.make_async_remote_copy(
+            src_ref=piece,
+            dst_ref=piece,
+            send_sem=send_sem.at[PARTNER, chip, h],
+            recv_sem=pair_recv.at[chip, h],
+            device_id=targets[PARTNER],
+            device_id_type=MESH,
+        ).wait_recv()
+
+    def start(route, chip, h):
+        hop(route, chip, h).start()
+
+    def finish(route, chip, h):
+        hop(route, chip, h).wait_send()
+
+    def own_sends(act):
+        chip = z * 2 + x
+        pl.when(has_up)(lambda: act(UP, chip, group))
+        pl.when(has_down)(lambda: act(DOWN, chip, group))
+        act(ACROSS, chip, group)
+        act(ACROSS, chip, 1 - group)
+        act(PARTNER, chip, 0)
+        act(PARTNER, chip, 1)
+
+    def at_distance(distance, do):
+        for sign in (-1, 1):
+            plane = z + sign * distance
+            exists = plane >= 0 if sign < 0 else plane < planes
+            pl.when(exists)(functools.partial(do, plane, sign))
+
+    def line_step(distance, first, act):
+        def do(plane, sign):
+            chip = plane * 2 + x
+            if first:
+                arrive(chip, group)
+            if sign < 0:
+                pl.when(has_up)(lambda: act(UP, chip, group))
+            else:
+                pl.when(has_down)(lambda: act(DOWN, chip, group))
+            act(OVER, chip, group)
+            act(ACROSS, chip, group)
+            act(PARTNER, chip, group)
+
+        at_distance(distance, do)
+
+    def across_own(first, act):
+        chip = z * 2 + 1 - x
+        for h in (group, 1 - group):
+            if first:
+                arrive(chip, h)
+            act(PARTNER, chip, h)
+
+    def plane_step(distance, first, act):
+        def do(plane, sign):
+            far, near = plane * 2 + 1 - x, plane * 2 + x
+            if first:
+                arrive(far, group)
+            act(OVER, far, group)
+            act(PARTNER, far, group)
+            if first:
+                arrive(near, 1 - group)
+            act(PARTNER, near, 1 - group)
+
+        at_distance(distance, do)
+
+    def corner_step(distance, first, act):
+        def do(plane, sign):
+            chip = plane * 2 + 1 - x
+            if first:
+                arrive(chip, 1 - group)
+            act(PARTNER, chip, 1 - group)
+
+        at_distance(distance, do)
+
+    def attend(slot):
+        def one_head(head, carry):
+            lanes = pl.ds(pl.multiple_of(head * head_dim, head_dim), head_dim)
+            query = held_queries[slot, :, lanes]
+            scores = [
+                lax.dot_general(
+                    query,
+                    ext_keys[places_ref[slot, j], :, lanes],
+                    NT,
+                    preferred_element_type=jnp.float32,
+                )
+                * (1.0 / math.sqrt(head_dim))
+                + bias_ref[slot, j]
+                for j in range(3)
+            ]
+            row_max = jnp.max(
+                jnp.maximum(jnp.maximum(scores[0], scores[1]), scores[2]), axis=-1, keepdims=True
+            )
+            raw = [jnp.exp(s - row_max) for s in scores]
+            denominator = jnp.sum(raw[0] + raw[1] + raw[2], axis=-1, keepdims=True)
+            summed = sum(
+                jnp.dot(
+                    raw[j].astype(jnp.bfloat16),
+                    ext_values[places_ref[slot, j], :, lanes],
+                    preferred_element_type=jnp.float32,
+                )
+                for j in range(3)
+            )
+            scaled = summed / denominator * gates_ref[slot, :, lanes]
+            attended[pl.ds(slot * rows, rows), lanes] = scaled.astype(jnp.bfloat16)
+            return carry
+
+        lax.fori_loop(0, HEADS, one_head, 0, unroll=2)
+
+    def project(chip):
+        for h in range(2):
+            arrive_pair(chip, h)
+        columns = 2 * gathered.shape[3]
+        total = sum(
+            lax.dot_general(
+                attended[:, h * half : (h + 1) * half],
+                gathered[chip, h].reshape(columns, half),
+                NT,
+                preferred_element_type=jnp.float32,
+            )
+            for h in range(2)
+        )
+        out_ref[:, pl.ds(pl.multiple_of(chip * columns, columns), columns)] = total.astype(
+            out_ref.dtype
+        )
+
+    for load in loads[:2]:
+        load.wait()
+    own_sends(start)
+    for load in loads[2:]:
+        load.wait()
+    line_step(1, True, start)
+    across_own(True, start)
+    for copy in halos:
+        copy.wait_recv()
+    attend(0)
+    for distance in range(2, planes):
+        line_step(distance, True, start)
+        if distance < slots + 1:
+            attend(distance - 1)
+        plane_step(distance - 1, True, start)
+    for slot in range(planes - 1, slots):
+        attend(slot)
+    plane_step(planes - 1, True, start)
+    project(z * 2 + 1 - x)
+
+    def near_unit(plane, carry):
+        project(plane * 2 + x)
+        return carry
+
+    lax.fori_loop(0, planes, near_unit, 0)
+    for distance in range(1, planes):
+        corner_step(distance, True, start)
+
+    def far_unit(i, carry):
+        plane = lax.rem(z + i, planes)
+        project(plane * 2 + 1 - x)
+        return carry
+
+    lax.fori_loop(1, planes, far_unit, 0)
+
+    own_sends(finish)
+    across_own(False, finish)
+    for distance in range(1, planes):
+        line_step(distance, False, finish)
+        plane_step(distance, False, finish)
+        corner_step(distance, False, finish)
+    for copy in halos:
+        copy.wait_send()
+
+
+def fits(mesh):
+    return mesh.shape["groups"] == 2 and mesh.shape["dp"] in (8, 16)
+
+
+def on_device_fused(mesh, queries, keys, values, counts, neighbours, gate_table, step, out_weight):
+    slots, rows, channels = queries.shape
+    planes = mesh.shape["dp"] // 4
+    columns = out_weight.shape[1]
+    if 2 * columns % 128 or columns % 16:
+        return on_device(queries, keys, values, counts, neighbours, gate_table, step, out_weight)
+    sentinel = slots + 2 * HALO
+    tail_start = jnp.maximum(counts[0] - HALO, 0)
+    tail_keys = lax.dynamic_slice_in_dim(keys, tail_start, HALO, 0)
+    tail_values = lax.dynamic_slice_in_dim(values, tail_start, HALO, 0)
+    half = channels // 2
+    weight = jnp.transpose(out_weight.reshape(2, half, columns), (0, 2, 1))
+    gate_row = lax.dynamic_index_in_dim(gate_table, step[0], 0, keepdims=False)
+    live = (jnp.arange(slots) < counts[0]).astype(jnp.float32)
+    gates = live[:, None, None] * gate_row[None, None, :]
+    bias = jnp.where(neighbours == sentinel, masked_score, 0.0).astype(jnp.float32)
+    bias = jnp.broadcast_to(bias[:, :, None, None], (slots, neighbours.shape[1], 1, rows))
+    places = jnp.minimum(neighbours, sentinel - 1)
+    chips = planes * 2
+    anywhere = pl.BlockSpec(memory_space=pl.ANY)
+    vmem = pl.BlockSpec(memory_space=pltpu.VMEM)
+    out = pl.pallas_call(
+        functools.partial(fused, planes),
+        out_shape=jax.ShapeDtypeStruct((slots * rows, chips * 2 * columns), jnp.bfloat16),
+        in_specs=[anywhere] * 6 + [vmem, vmem, pl.BlockSpec(memory_space=pltpu.SMEM)],
+        out_specs=vmem,
+        scratch_shapes=[
+            pltpu.VMEM((sentinel, rows, channels), jnp.bfloat16),
+            pltpu.VMEM((sentinel, rows, channels), jnp.bfloat16),
+            pltpu.VMEM((slots, rows, channels), jnp.bfloat16),
+            pltpu.VMEM((slots * rows, channels), jnp.bfloat16),
+            pltpu.VMEM((chips, 2, 2, columns, half), jnp.bfloat16),
+            pltpu.SemaphoreType.DMA((5,)),
+            pltpu.SemaphoreType.DMA((4,)),
+            pltpu.SemaphoreType.DMA((4,)),
+            pltpu.SemaphoreType.DMA((5, chips, 2)),
+            pltpu.SemaphoreType.DMA((chips, 2)),
+            pltpu.SemaphoreType.DMA((chips, 2)),
+        ],
+        compiler_params=pltpu.CompilerParams(
+            collective_id=0, has_side_effects=True, vmem_limit_bytes=60 * 2**20
+        ),
+        name="fused",
+    )(keys, values, queries, tail_keys, tail_values, weight, gates, bias, places)
+    return out.reshape(slots, rows, -1)
+
+
 def solution(mesh):
     placed = (
         P(("groups", "dp"), None, None),
@@ -86,7 +422,7 @@
         P(None, "dp"),
     )
     return jax.shard_map(
-        on_device,
+        functools.partial(on_device_fused, mesh) if fits(mesh) else on_device,
         mesh=mesh,
         in_specs=placed,
         out_specs=P(("groups", "dp"), None, None),

time: 205 us -> 176 us (0.86)
  the two profiles are of different devices: /device:TPU:5 before, /device:TPU:3 now
where the time goes in v1:
time: 176 us
  Pallas kernels  163 us (93%)
  local copies, waits for them, and re-layouts  8.73 us (5%)
  other arithmetic  2.63 us (1%)
    pallas_call x1, Pallas kernels, on_device_fused(): pl.pallas_call(functools.partial(fused, planes), out_shape=jax.ShapeDtype...  163 us
    unnamed x5, local copies, waits for them, and re-layouts  4.3 us

profile of v1, /device:TPU:3, one launch (start us, length us, event | category | flops | bytes accessed | tf_op | source)
XLA Modules:
  0.0 176.1 jit_solution(11068842401861331279)
XLA Ops:
  0.0 0.0 copy-start
  0.0 0.0 copy-start.1
  1.5 1.2 broadcast_minimum_fusion.places_ref
  2.7 0.7 compare_select_fusion
  3.4 0.7 broadcast_in_dim.18.bias_ref
  4.1 0.0 copy-done
  4.1 0.7 broadcast_multiply_fusion.gates_ref
  4.8 2.5 %constant_dynamic-slice_fusion = (bf16[1,128,2560]{2,1,0:T(8,128)(2,1)}, bf16[1,128,2560]{2,1,0:T(8,128)(2,1)}) fusion(bf16[3,128,2560]{2,1,0:T(8,128)(2,1)} %values_hbm.1, s32[]{:T(128)S(6)} %max.3, bf16[3,128,2560]{2,1,0:T(8,128)(2,1)} %keys_hbm.1), kind=kLoop, calls=%fused_computation.6 | loop fusion | bytes 2621444 | tf_op jit(solution)/shard_map/dynamic_slice | solution.py:375
  7.3 0.0 copy-done.1
  7.3 1.3 copy.12
  8.5 163.3 %fused.1 = bf16[384,5120]{1,0:T(8,128)(2,1)} custom-call(bf16[3,128,2560]{2,1,0:T(8,128)(2,1)} %keys_hbm.1, bf16[3,128,2560]{2,1,0:T(8,128)(2,1)} %values_hbm.1, bf16[3,128,2560]{2,1,0:T(8,128)(2,1)} %queries_hbm.1, bf16[1,128,2560]{2,1,0:T(8,128)(2,1)} %get-tuple-element.6.tail_keys, bf16[1,128,2560]{2,1,0:T(8,128)(2,1)} %get-tuple-element.5.tail_values, ...), custom_call_target="tpu_custom_call" | custom-call | tf_op jit(solution)/shard_map/fused/pallas_call | solution.py:387
  171.8 4.3 %copy.16 = bf16[3,128,5120]{2,1,0:T(8,128)(2,1)} copy(bf16[3,128,5120]{2,1,0:T(8,128)(2,1)} %bitcast.15) | data formatting | bytes 7864320
  (2 shorter events, 0.0 us)
Async XLA Ops:
  0.0 4.1 %copy-start = (f32[50,2560]{1,0:T(8,128)S(1)}, f32[50,2560]{1,0:T(8,128)}, u32[]{:S(2)}) copy-start(f32[50,2560]{1,0:T(8,128)} %param.13) | copy-start | bytes 1536004
  0.0 7.3 %copy-start.1 = (bf16[2560,320]{0,1:T(8,128)(2,1)S(1)}, bf16[2560,320]{0,1:T(8,128)(2,1)}, u32[]{:S(2)}) copy-start(bf16[2560,320]{0,1:T(8,128)(2,1)} %param.15) | copy-start | bytes 4915204

commit v2 on v1

--- a/solution.py
+++ b/solution.py
@@ -80,6 +80,9 @@
 MESH = pl.DeviceIdType.MESH
 NT = (((1,), (1,)), ((), ()))
 UP, DOWN, ACROSS, OVER, PARTNER = range(5)
+PARTS = 2
+RELAYED = 2
+CORNER_OVER = 0
 
 
 def fused(
@@ -169,49 +172,62 @@
         halo(2, tail_values, ext_values.at[pl.ds(0, HALO)], after),
         halo(3, values_hbm.at[pl.ds(0, HALO)], ext_values.at[pl.ds(HALO + slots, HALO)], before),
     ]
-    for copy in halos:
-        copy.start()
-
-    def hop(route, chip, h):
-        piece = gathered.at[chip, h, core]
+
+    span = gathered.shape[3] // PARTS
+    mate = z + 1 - 2 * lax.rem(z, 2)
+
+    def hop(route, chip, h, s):
+        piece = gathered.at[chip, h, core, pl.ds(s * span, span)]
         recv = pair_recv if route == PARTNER else class_recv
         return pltpu.make_async_remote_copy(
             src_ref=piece,
             dst_ref=piece,
-            send_sem=send_sem.at[route, chip, h],
-            recv_sem=recv.at[chip, h],
+            send_sem=send_sem.at[route, chip, h, s],
+            recv_sem=recv.at[chip, h, s],
             device_id=targets[route],
             device_id_type=MESH,
         )
 
-    def arrive(chip, h):
-        hop(ACROSS, chip, h).wait_recv()
-
-    def arrive_pair(chip, h):
-        piece = gathered.at[chip, h, 1 - core]
+    def arrive(chip, h, s):
+        hop(ACROSS, chip, h, s).wait_recv()
+
+    def arrive_pair(chip, h, s):
+        piece = gathered.at[chip, h, 1 - core, pl.ds(s * span, span)]
         pltpu.make_async_remote_copy(
             src_ref=piece,
             dst_ref=piece,
-            send_sem=send_sem.at[PARTNER, chip, h],
-            recv_sem=pair_recv.at[chip, h],
+            send_sem=send_sem.at[PARTNER, chip, h, s],
+            recv_sem=pair_recv.at[chip, h, s],
             device_id=targets[PARTNER],
             device_id_type=MESH,
         ).wait_recv()
 
-    def start(route, chip, h):
-        hop(route, chip, h).start()
-
-    def finish(route, chip, h):
-        hop(route, chip, h).wait_send()
-
-    def own_sends(act):
+    def start(route, chip, h, s):
+        hop(route, chip, h, s).start()
+
+    def finish(route, chip, h, s):
+        hop(route, chip, h, s).wait_send()
+
+    def own_line(act):
         chip = z * 2 + x
-        pl.when(has_up)(lambda: act(UP, chip, group))
-        pl.when(has_down)(lambda: act(DOWN, chip, group))
-        act(ACROSS, chip, group)
-        act(ACROSS, chip, 1 - group)
-        act(PARTNER, chip, 0)
-        act(PARTNER, chip, 1)
+        for s in range(PARTS):
+            pl.when(has_up)(lambda: act(UP, chip, group, s))
+            pl.when(has_down)(lambda: act(DOWN, chip, group, s))
+            act(ACROSS, chip, group, s)
+
+    def own_rest(act):
+        for s in range(PARTS):
+            act(ACROSS, z * 2 + x, 1 - group, s)
+
+    def own_pair(act):
+        for h in range(2):
+            for s in range(PARTS):
+                act(PARTNER, z * 2 + x, h, s)
+
+    def relay(h, s, act):
+        chip = z * 2 + 1 - x
+        pl.when(mate > z)(lambda: act(UP, chip, h, s))
+        pl.when(mate < z)(lambda: act(DOWN, chip, h, s))
 
     def at_distance(distance, do):
         for sign in (-1, 1):
@@ -220,46 +236,83 @@
             pl.when(exists)(functools.partial(do, plane, sign))
 
     def line_step(distance, first, act):
-        def do(plane, sign):
-            chip = plane * 2 + x
+        for s in range(PARTS):
+
+            def do(plane, sign):
+                chip = plane * 2 + x
+                if first:
+                    arrive(chip, group, s)
+                if sign < 0:
+                    pl.when(has_up)(lambda: act(UP, chip, group, s))
+                else:
+                    pl.when(has_down)(lambda: act(DOWN, chip, group, s))
+                act(OVER, chip, group, s)
+                if s < RELAYED:
+                    pl.when(plane != mate)(lambda: act(ACROSS, chip, group, s))
+                else:
+                    act(ACROSS, chip, group, s)
+                act(PARTNER, chip, group, s)
+
+            at_distance(distance, do)
+
+    def across_own(first, act):
+        for s in range(PARTS):
             if first:
-                arrive(chip, group)
-            if sign < 0:
-                pl.when(has_up)(lambda: act(UP, chip, group))
-            else:
-                pl.when(has_down)(lambda: act(DOWN, chip, group))
-            act(OVER, chip, group)
-            act(ACROSS, chip, group)
-            act(PARTNER, chip, group)
-
-        at_distance(distance, do)
-
-    def across_own(first, act):
-        chip = z * 2 + 1 - x
-        for h in (group, 1 - group):
+                arrive(z * 2 + 1 - x, group, s)
+            act(PARTNER, z * 2 + 1 - x, group, s)
+
+    def relay_own(act):
+        for s in range(RELAYED):
+            relay(group, s, act)
+
+    def across_rest(first, act):
+        for s in range(PARTS):
             if first:
-                arrive(chip, h)
-            act(PARTNER, chip, h)
-
-    def plane_step(distance, first, act):
-        def do(plane, sign):
-            far, near = plane * 2 + 1 - x, plane * 2 + x
-            if first:
-                arrive(far, group)
-            act(OVER, far, group)
-            act(PARTNER, far, group)
-            if first:
-                arrive(near, 1 - group)
-            act(PARTNER, near, 1 - group)
-
-        at_distance(distance, do)
+                arrive(z * 2 + 1 - x, 1 - group, s)
+            if s >= CORNER_OVER:
+                relay(1 - group, s, act)
+            act(PARTNER, z * 2 + 1 - x, 1 - group, s)
+
+    def near_step(distance, first, act):
+        for s in range(PARTS):
+
+            def do(plane, sign):
+                if first:
+                    arrive(plane * 2 + x, 1 - group, s)
+                act(PARTNER, plane * 2 + x, 1 - group, s)
+
+            at_distance(distance, do)
+
+    def far_piece(chip, s, over, first, act):
+        if first:
+            arrive(chip, group, s)
+        if over:
+            act(OVER, chip, group, s)
+        act(PARTNER, chip, group, s)
+
+    def far_step(distance, first, act):
+        for s in range(PARTS):
+
+            def do(plane, sign):
+                pl.when(plane != mate)(
+                    lambda: far_piece(plane * 2 + 1 - x, s, True, first, act)
+                )
+
+            at_distance(distance, do)
+
+    def mate_step(first, act):
+        for s in range(PARTS):
+            far_piece(mate * 2 + 1 - x, s, s < CORNER_OVER, first, act)
 
     def corner_step(distance, first, act):
         def do(plane, sign):
             chip = plane * 2 + 1 - x
+            for s in range(PARTS):
+                if first:
+                    arrive(chip, 1 - group, s)
+                act(PARTNER, chip, 1 - group, s)
             if first:
-                arrive(chip, 1 - group)
-            act(PARTNER, chip, 1 - group)
+                project(chip)
 
         at_distance(distance, do)
 
@@ -299,7 +352,8 @@
 
     def project(chip):
         for h in range(2):
-            arrive_pair(chip, h)
+            for s in range(PARTS):
+                arrive_pair(chip, h, s)
         columns = 2 * gathered.shape[3]
         total = sum(
             lax.dot_general(
@@ -316,44 +370,57 @@
 
     for load in loads[:2]:
         load.wait()
-    own_sends(start)
+    edge = jnp.logical_or(z == 0, z == planes - 1)
+    inner = jnp.logical_not(edge)
+    own_line(start)
+    for copy in halos:
+        copy.start()
+    own_pair(start)
+    line_step(1, True, start)
+    across_own(True, start)
     for load in loads[2:]:
         load.wait()
-    line_step(1, True, start)
-    across_own(True, start)
+    for distance in range(2, planes):
+        line_step(distance, True, start)
+        if distance == 2:
+            pl.when(inner)(lambda: own_rest(start))
+            relay_own(start)
+    pl.when(edge)(lambda: own_rest(start))
+    if planes == 2:
+        relay_own(start)
     for copy in halos:
         copy.wait_recv()
     attend(0)
-    for distance in range(2, planes):
-        line_step(distance, True, start)
-        if distance < slots + 1:
-            attend(distance - 1)
-        plane_step(distance - 1, True, start)
-    for slot in range(planes - 1, slots):
+    for distance in range(1, planes):
+        near_step(distance, True, start)
+        far_step(distance, True, start)
+        if distance < slots:
+            attend(distance)
+    for slot in range(planes, slots):
         attend(slot)
-    plane_step(planes - 1, True, start)
-    project(z * 2 + 1 - x)
 
     def near_unit(plane, carry):
         project(plane * 2 + x)
         return carry
 
     lax.fori_loop(0, planes, near_unit, 0)
-    for distance in range(1, planes):
+    mate_step(True, start)
+    across_rest(True, start)
+    project(z * 2 + 1 - x)
+    for distance in range(planes - 1, 0, -1):
         corner_step(distance, True, start)
 
-    def far_unit(i, carry):
-        plane = lax.rem(z + i, planes)
-        project(plane * 2 + 1 - x)
-        return carry
-
-    lax.fori_loop(1, planes, far_unit, 0)
-
-    own_sends(finish)
+    own_line(finish)
+    own_rest(finish)
+    own_pair(finish)
     across_own(False, finish)
+    relay_own(finish)
+    across_rest(False, finish)
+    mate_step(False, finish)
     for distance in range(1, planes):
         line_step(distance, False, finish)
-        plane_step(distance, False, finish)
+        near_step(distance, False, finish)
+        far_step(distance, False, finish)
         corner_step(distance, False, finish)
     for copy in halos:
         copy.wait_send()
@@ -367,7 +434,7 @@
     slots, rows, channels = queries.shape
     planes = mesh.shape["dp"] // 4
     columns = out_weight.shape[1]
-    if 2 * columns % 128 or columns % 16:
+    if 2 * columns % 128 or columns % (16 * PARTS):
         return on_device(queries, keys, values, counts, neighbours, gate_table, step, out_weight)
     sentinel = slots + 2 * HALO
     tail_start = jnp.maximum(counts[0] - HALO, 0)
@@ -398,9 +465,9 @@
             pltpu.SemaphoreType.DMA((5,)),
             pltpu.SemaphoreType.DMA((4,)),
             pltpu.SemaphoreType.DMA((4,)),
-            pltpu.SemaphoreType.DMA((5, chips, 2)),
-            pltpu.SemaphoreType.DMA((chips, 2)),
-            pltpu.SemaphoreType.DMA((chips, 2)),
+            pltpu.SemaphoreType.DMA((5, chips, 2, PARTS)),
+            pltpu.SemaphoreType.DMA((chips, 2, PARTS)),
+            pltpu.SemaphoreType.DMA((chips, 2, PARTS)),
         ],
         compiler_params=pltpu.CompilerParams(
             collective_id=0, has_side_effects=True, vmem_limit_bytes=60 * 2**20

time: 176 us -> 152 us (0.86)
  Pallas kernels: 163 us -> 139 us
    pallas_call x1, Pallas kernels: 163 us -> 139 us  [on_device_fused(): pl.pallas_call(functools.partial(fused, planes), out_shape=jax.ShapeDtype...]
where the time goes in v2:
time: 152 us
  Pallas kernels  139 us (91%)
  local copies, waits for them, and re-layouts  8.73 us (6%)
  other arithmetic  2.63 us (2%)
    pallas_call x1, Pallas kernels, on_device_fused(): pl.pallas_call(functools.partial(fused, planes), out_shape=jax.ShapeDtype...  139 us
    unnamed x5, local copies, waits for them, and re-layouts  4.3 us

profile of v2, /device:TPU:3, one launch (start us, length us, event | category | flops | bytes accessed | tf_op | source)
XLA Modules:
  0.0 151.9 jit_solution(5430349568435559084)
XLA Ops:
  0.0 0.0 copy-start
  0.0 0.0 copy-start.1
  1.5 1.2 broadcast_minimum_fusion.places_ref
  2.7 0.7 compare_select_fusion
  3.4 0.7 broadcast_in_dim.18.bias_ref
  4.1 0.0 copy-done
  4.1 0.7 broadcast_multiply_fusion.gates_ref
  4.8 2.5 %constant_dynamic-slice_fusion = (bf16[1,128,2560]{2,1,0:T(8,128)(2,1)}, bf16[1,128,2560]{2,1,0:T(8,128)(2,1)}) fusion(bf16[3,128,2560]{2,1,0:T(8,128)(2,1)} %values_hbm.1, s32[]{:T(128)S(6)} %max.3, bf16[3,128,2560]{2,1,0:T(8,128)(2,1)} %keys_hbm.1), kind=kLoop, calls=%fused_computation.6 | loop fusion | bytes 2621444 | tf_op jit(solution)/shard_map/dynamic_slice | solution.py:442
  7.3 0.0 copy-done.1
  7.3 1.3 copy.12
  8.5 139.1 %fused.1 = bf16[384,5120]{1,0:T(8,128)(2,1)} custom-call(bf16[3,128,2560]{2,1,0:T(8,128)(2,1)} %keys_hbm.1, bf16[3,128,2560]{2,1,0:T(8,128)(2,1)} %values_hbm.1, bf16[3,128,2560]{2,1,0:T(8,128)(2,1)} %queries_hbm.1, bf16[1,128,2560]{2,1,0:T(8,128)(2,1)} %get-tuple-element.6.tail_keys, bf16[1,128,2560]{2,1,0:T(8,128)(2,1)} %get-tuple-element.5.tail_values, ...), custom_call_target="tpu_custom_call" | custom-call | tf_op jit(solution)/shard_map/fused/pallas_call | solution.py:454
  147.6 4.3 %copy.16 = bf16[3,128,5120]{2,1,0:T(8,128)(2,1)} copy(bf16[3,128,5120]{2,1,0:T(8,128)(2,1)} %bitcast.15) | data formatting | bytes 7864320
  (2 shorter events, 0.0 us)
Async XLA Ops:
  0.0 4.1 %copy-start = (f32[50,2560]{1,0:T(8,128)S(1)}, f32[50,2560]{1,0:T(8,128)}, u32[]{:S(2)}) copy-start(f32[50,2560]{1,0:T(8,128)} %param.13) | copy-start | bytes 1536004
  0.0 7.3 %copy-start.1 = (bf16[2560,320]{0,1:T(8,128)(2,1)S(1)}, bf16[2560,320]{0,1:T(8,128)(2,1)}, u32[]{:S(2)}) copy-start(bf16[2560,320]{0,1:T(8,128)(2,1)} %param.15) | copy-start | bytes 4915204

commit v3 on v2

--- a/solution.py
+++ b/solution.py
@@ -348,7 +348,7 @@
             attended[pl.ds(slot * rows, rows), lanes] = scaled.astype(jnp.bfloat16)
             return carry
 
-        lax.fori_loop(0, HEADS, one_head, 0, unroll=2)
+        lax.fori_loop(0, HEADS, one_head, 0, unroll=4)
 
     def project(chip):
         for h in range(2):
@@ -407,7 +407,7 @@
     mate_step(True, start)
     across_rest(True, start)
     project(z * 2 + 1 - x)
-    for distance in range(planes - 1, 0, -1):
+    for distance in (*range(2, planes), 1):
         corner_step(distance, True, start)
 
     own_line(finish)

time: 152 us -> 148 us (0.974); the launches traced: 152 us -> 145 us
  Pallas kernels: 139 us -> 132 us
    pallas_call x1, Pallas kernels: 139 us -> 132 us  [on_device_fused(): pl.pallas_call(functools.partial(fused, planes), out_shape=jax.ShapeDtype...]
where the time goes in v3:
time: 148 us; the launch traced here: 145 us
  Pallas kernels  132 us (89%)
  local copies, waits for them, and re-layouts  8.73 us (6%)
  other arithmetic  2.63 us (2%)
  between operations  1.48 us (1%)
    pallas_call x1, Pallas kernels, on_device_fused(): pl.pallas_call(functools.partial(fused, planes), out_shape=jax.ShapeDtype...  132 us
    unnamed x5, local copies, waits for them, and re-layouts  4.3 us

profile of v3, /device:TPU:3, one launch (start us, length us, event | category | flops | bytes accessed | tf_op | source)
XLA Modules:
  0.0 144.9 jit_solution(10969880715367256843)
XLA Ops:
  0.0 0.0 copy-start
  0.0 0.0 copy-start.1
  1.5 1.2 broadcast_minimum_fusion.places_ref
  2.7 0.7 compare_select_fusion
  3.4 0.7 broadcast_in_dim.18.bias_ref
  4.1 0.0 copy-done
  4.1 0.7 broadcast_multiply_fusion.gates_ref
  4.8 2.5 %constant_dynamic-slice_fusion = (bf16[1,128,2560]{2,1,0:T(8,128)(2,1)}, bf16[1,128,2560]{2,1,0:T(8,128)(2,1)}) fusion(bf16[3,128,2560]{2,1,0:T(8,128)(2,1)} %values_hbm.1, s32[]{:T(128)S(6)} %max.3, bf16[3,128,2560]{2,1,0:T(8,128)(2,1)} %keys_hbm.1), kind=kLoop, calls=%fused_computation.6 | loop fusion | bytes 2621444 | tf_op jit(solution)/shard_map/dynamic_slice | solution.py:442
  7.3 0.0 copy-done.1
  7.3 1.3 copy.12
  8.5 132.1 %fused.1 = bf16[384,5120]{1,0:T(8,128)(2,1)} custom-call(bf16[3,128,2560]{2,1,0:T(8,128)(2,1)} %keys_hbm.1, bf16[3,128,2560]{2,1,0:T(8,128)(2,1)} %values_hbm.1, bf16[3,128,2560]{2,1,0:T(8,128)(2,1)} %queries_hbm.1, bf16[1,128,2560]{2,1,0:T(8,128)(2,1)} %get-tuple-element.6.tail_keys, bf16[1,128,2560]{2,1,0:T(8,128)(2,1)} %get-tuple-element.5.tail_values, ...), custom_call_target="tpu_custom_call" | custom-call | tf_op jit(solution)/shard_map/fused/pallas_call | solution.py:454
  140.6 4.3 %copy.16 = bf16[3,128,5120]{2,1,0:T(8,128)(2,1)} copy(bf16[3,128,5120]{2,1,0:T(8,128)(2,1)} %bitcast.15) | data formatting | bytes 7864320
  (2 shorter events, 0.0 us)
Async XLA Ops:
  0.0 4.1 %copy-start = (f32[50,2560]{1,0:T(8,128)S(1)}, f32[50,2560]{1,0:T(8,128)}, u32[]{:S(2)}) copy-start(f32[50,2560]{1,0:T(8,128)} %param.13) | copy-start | bytes 1536004
  0.0 7.3 %copy-start.1 = (bf16[2560,320]{0,1:T(8,128)(2,1)S(1)}, bf16[2560,320]{0,1:T(8,128)(2,1)}, u32[]{:S(2)}) copy-start(bf16[2560,320]{0,1:T(8,128)(2,1)} %param.15) | copy-start | bytes 4915204
